TPU v7x, 32 devices: a whole 2x2x4 slice. The times are simulated.
32 devices in a mesh: rows: 8 (over z, y), cls: 4 (over x, core).
Axes of the slice: x: 2, y: 2, z: 4, core: 2. Of those that a mesh axis runs over, the one named last changes fastest.
Arguments:
- features: bfloat16 [6144, 2048], P('rows', 'cls'), may hold values from -32 to 32
- prototypes: bfloat16 [2048, 16384], P('rows', 'cls'), may hold values from -1 to 1
Outputs:
- grad_proto: float32 [2048, 16384], P('rows', 'cls')
All inputs are finite; a program needn't handle non-finite values.
Results may differ from a plain program's by a relative error of at most 0.02.
Values may be sent and summed in bfloat16 or wider, within the bound.
A program may use at most 128 MiB of HBM per device.

v0:
```python
import jax
import jax.numpy as jnp
from jax import lax
from jax.sharding import PartitionSpec as P

ITERS = 3


code_temp = 0.2
loss_temp = 0.3


def local(features, prototypes):
    gathered = lax.all_gather(features, "cls", axis=1, tiled=True)
    local_rows = gathered.shape[0]
    local_classes = prototypes.shape[1]
    balance_ratio = float(local_rows * lax.axis_size("rows")) / float(
        local_classes * lax.axis_size("cls")
    )
    columns = gathered
    scores = jnp.dot(
        columns,
        lax.all_gather(prototypes, "rows", axis=0, tiled=True),
        preferred_element_type=jnp.float32,
    )
    local_top = jnp.max(scores, axis=1)
    row_top = lax.pmax(local_top, "cls")
    shifted = scores - row_top[:, None]
    exp_codes = jnp.exp(shifted / code_temp)
    exp_loss = jnp.exp(shifted / loss_temp)
    sink_total, soft_total = lax.psum(
        (jnp.sum(exp_codes, axis=1), jnp.sum(exp_loss, axis=1)), "cls"
    )
    codes = exp_codes / sink_total[:, None]
    for sweep in range(ITERS):
        col_mass = lax.psum(jnp.sum(codes, axis=0), "rows")
        codes = codes * (balance_ratio / col_mass)[None, :]
        row_mass = lax.psum(jnp.sum(codes, axis=1), "cls")
        codes = codes / row_mass[:, None]
    probs_loss = exp_loss / soft_total[:, None]
    slope = ((probs_loss - codes) / loss_temp).astype(jnp.bfloat16)
    columns = gathered
    return lax.psum_scatter(
        lax.dot_general(
            columns, slope, (((0,), (0,)), ((), ())), preferred_element_type=jnp.float32
        ).astype(jnp.bfloat16),
        "rows",
        scatter_dimension=0,
        tiled=True,
    ).astype(jnp.float32)


def solution(mesh):
    return jax.shard_map(
        local,
        mesh=mesh,
        in_specs=(P("rows", "cls"), P("rows", "cls")),
        out_specs=P("rows", "cls"),
        check_vma=False,
    )
```

profile of v0, /device:TPU:13, one launch (start us, length us, event | category | flops | bytes accessed | tf_op | source)
XLA Modules:
  0.0 783.0 jit_solution(6704144554605490783)
XLA Ops:
  6.5 0.0 all-gather.3.cloned.1.call-start
  6.5 0.7 all-gather.3.cloned.1.call-update
  7.3 0.0 all-gather.5.cloned.1.call-start
  7.3 0.7 all-gather.5.cloned.1.call-update
  8.0 0.0 reduce-scatter.2.cloned.1.call-start
  8.1 31.0 %all-gather.3.cloned.1.call-done = bf16[768,2048]{1,0:T(8,128)(2,1)} async-done(((bf16[768,512]{1,0:T(8,128)(2,1)}), bf16[768,2048]{1,0:T(8,128)(2,1)}) %all-gather.3.cloned.1.call-update) | async-done | bytes 3145744 | tf_op jit(solution)/shard_map/all_gather | solution.py:14
  39.0 226.3 %all-gather.5.cloned.1.call-done = bf16[2048,4096]{1,0:T(8,128)(2,1)} async-done(((bf16[256,4096]{1,0:T(8,128)(2,1)}), bf16[2048,4096]{1,0:T(8,128)(2,1)}) %all-gather.5.cloned.1.call-update) | async-done | bytes 16777232 | tf_op jit(solution)/shard_map/all_gather | solution.py:23
  265.3 20.3 %fusion.8 = (f32[768]{0:T(1024)S(1)}, f32[768,4096]{1,0:T(8,128)}) fusion(bf16[768,2048]{1,0:T(8,128)(2,1)} %all-gather.3.cloned.1.call-done, bf16[2048,4096]{1,0:T(8,128)(2,1)} %all-gather.5.cloned.1.call-done), kind=kOutput, calls=%fused_computation.19 | convolution fusion | flops 12888046592 | bytes 32508928 | tf_op jit(solution)/shard_map/dot_general | solution.py:21
  285.6 5.9 pmax.7
  291.5 7.1 fusion
  298.7 6.2 psum.57
  304.9 11.3 %fusion.6 = (f32[4096]{0:T(1024)S(1)}, f32[768,4096]{1,0:T(8,128)}) fusion(f32[768]{0:T(1024)S(1)} %psum.57, f32[768,4096]{1,0:T(8,128)} %get-tuple-element.14, f32[768]{0:T(1024)S(1)} %pmax.7), kind=kLoop, calls=%fused_computation.18 | loop fusion | flops 12578816 | bytes 25188352 | tf_op jit(solution)/shard_map/reduce_sum | solution.py:36
  316.2 24.4 %psum.58 = f32[4096]{0:T(1024)S(1)} all-reduce(f32[4096]{0:T(1024)S(1)} %get-tuple-element.11), channel_id=1, replica_groups=mesh['rows'=8,'cls'=4] {'rows'}, use_global_device_ids=true, to_apply=%region_7.0 | all-reduce | flops 4096 | bytes 32768 | tf_op jit(solution)/shard_map/psum | solution.py:36
  340.6 5.5 multiply_reduce_fusion.2
  346.1 13.3 %psum.59 = f32[768]{0:T(1024)S(1)} all-reduce(f32[768]{0:T(1024)S(1)} %multiply_reduce_fusion.2), channel_id=1, replica_groups=mesh['rows'=8,'cls'=4] {'cls'}, use_global_device_ids=true, to_apply=%region_9.0 | all-reduce | flops 768 | bytes 6144 | tf_op jit(solution)/shard_map/psum | solution.py:38
  359.4 6.4 fusion.4
  365.9 27.4 %psum.60 = f32[4096]{0:T(1024)S(1)} all-reduce(f32[4096]{0:T(1024)S(1)} %fusion.4), channel_id=1, replica_groups=mesh['rows'=8,'cls'=4] {'rows'}, use_global_device_ids=true, to_apply=%region_11.0 | all-reduce | flops 4096 | bytes 32768 | tf_op jit(solution)/shard_map/psum | solution.py:36
  393.3 6.0 multiply_reduce_fusion.1
  399.3 13.0 %psum.61 = f32[768]{0:T(1024)S(1)} all-reduce(f32[768]{0:T(1024)S(1)} %multiply_reduce_fusion.1), channel_id=1, replica_groups=mesh['rows'=8,'cls'=4] {'cls'}, use_global_device_ids=true, to_apply=%region_13.0 | all-reduce | flops 768 | bytes 6144 | tf_op jit(solution)/shard_map/psum | solution.py:38
  412.3 11.3 %fusion.5 = (f32[4096]{0:T(1024)S(1)}, f32[768,4096]{1,0:T(8,128)}) fusion(f32[768]{0:T(1024)S(1)} %psum.61, f32[4096]{0:T(1024)S(1)} %broadcast_divide_fusion.1, f32[768]{0:T(1024)S(1)} %psum.59, f32[768,4096]{1,0:T(8,128)} %get-tuple-element.12, f32[4096]{0:T(1024)S(1)} %broadcast_divide_fusion.2), kind=kLoop, calls=%fused_computation.17 | loop fusion | flops 15724544 | bytes 25221120 | tf_op jit(solution)/shard_map/reduce_sum | solution.py:36
  423.6 0.0 copy-start
  423.6 26.1 %psum.62 = f32[4096]{0:T(1024)S(1)} all-reduce(f32[4096]{0:T(1024)S(1)} %get-tuple-element.9), channel_id=1, replica_groups=mesh['rows'=8,'cls'=4] {'rows'}, use_global_device_ids=true, to_apply=%region_15.0 | all-reduce | flops 4096 | bytes 32768 | tf_op jit(solution)/shard_map/psum | solution.py:36
  449.7 5.5 multiply_reduce_fusion
  455.2 13.1 %all-reduce = (f32[768]{0:T(1024)S(1)}, f32[768]{0:T(1024)S(1)}) all-reduce(f32[768]{0:T(1024)S(1)} %multiply_reduce_fusion, f32[768]{0:T(1024)S(1)} %get-tuple-element.5), channel_id=1, replica_groups=mesh['rows'=8,'cls'=4] {'cls'}, use_global_device_ids=true, to_apply=%region_17.0 | all-reduce | flops 1536 | bytes 12288 | tf_op jit(solution)/shard_map/psum | solution.py:38
  468.3 0.0 copy-done
  468.3 22.6 %convert_bitcast_fusion = bf16[2048,4096]{0,1:T(8,128)(2,1)} fusion(bf16[768,2048]{1,0:T(8,128)(2,1)S(1)} %copy-done, f32[768,4096]{1,0:T(8,128)} %get-tuple-element.10, f32[768,4096]{1,0:T(8,128)} %get-tuple-element.14, f32[768]{0:T(1024)S(1)} %get-tuple-element.7, f32[4096]{0:T(1024)S(1)} %broadcast_divide_fusion, f32[768]{0:T(1024)S(1)} %get-tuple-element.8, ...), kind=kOutput, calls=%fused_computation | convolution fusion | flops 12918456320 | bytes 45114368 | tf_op jit(solution)/shard_map/dot_general | solution.py:44
  491.0 0.0 reduce-scatter.2.cloned.1.call-update
  491.0 281.2 %reduce-scatter.2.cloned.1.call-done = bf16[256,4096]{0,1:T(8,128)(2,1)} async-done(((bf16[2048,4096]{0,1:T(8,128)(2,1)}), bf16[256,4096]{0,1:T(8,128)(2,1)}) %reduce-scatter.2.cloned.1.call-update) | async-done | bytes 2097168 | tf_op jit(solution)/shard_map/reduce_scatter | solution.py:43
  772.2 4.3 copy.3
  (3 shorter events, 0.0 us)
Async XLA Ops:
  6.5 32.5 %all-gather.3.cloned.1.call-start = ((), (), s32[]{:S(2)}) async-start(), calls=%async_computation.1 | async-start | bytes 3932160 | tf_op jit(solution)/shard_map/all_gather | solution.py:14
  7.3 258.1 %all-gather.5.cloned.1.call-start = ((), (), s32[]{:S(2)}) async-start(), calls=%async_computation.2 | async-start | bytes 18874368 | tf_op jit(solution)/shard_map/all_gather | solution.py:23
  8.0 764.2 %reduce-scatter.2.cloned.1.call-start = ((), (), s32[]{:S(2)}) async-start(), calls=%async_computation.3 | async-start | bytes 18874368 | tf_op jit(solution)/shard_map/reduce_scatter | solution.py:43
  423.6 44.7 %copy-start = (bf16[768,2048]{1,0:T(8,128)(2,1)S(1)}, bf16[768,2048]{1,0:T(8,128)(2,1)}, u32[]{:S(2)}) copy-start(bf16[768,2048]{1,0:T(8,128)(2,1)} %all-gather.3.cloned.1.call-done) | copy-start | bytes 9437188
Sparse Core Ops, SparseCore 0:
  8.9 30.0 all-gather.2
  41.1 224.1 all-gather.4
  491.1 281.0 reduce-scatter.1
where the time goes:
time: 787 us; the launch traced here: 783 us
  waiting for transfers between devices  540 us (69%)
  blocking collectives  130 us (17%)
  other arithmetic  53.1 us (7%)
  matrix products  43 us (5%)
  between operations  13.1 us (2%)
    reduce_scatter x1, waiting for transfers between devices, local(): lax.psum_scatter(lax.dot_general(columns, slope, (((0,), (0,)), ((), ()))...  281 us
    all_gather x1, waiting for transfers between devices, local(): lax.all_gather(prototypes, 'rows', axis=0, tiled=True)  226 us
    psum x3, blocking collectives, local(): col_mass = lax.psum(jnp.sum(codes, axis=0), 'rows')  78 us
    psum x3, blocking collectives, local(): row_mass = lax.psum(jnp.sum(codes, axis=1), 'cls')  39.4 us
    all_gather x1, waiting for transfers between devices, local(): gathered = lax.all_gather(features, 'cls', axis=1, tiled=True)  31 us
    reduce_sum x3, other arithmetic, local(): col_mass = lax.psum(jnp.sum(codes, axis=0), 'rows')  29 us
    dot_general x1, matrix products, local(): lax.dot_general(columns, slope, (((0,), (0,)), ((), ())), preferred_eleme...  22.6 us
    dot_general x1, matrix products, local(): jnp.dot(columns, lax.all_gather(prototypes, 'rows', axis=0, tiled=True),...  20.3 us
  transfers between devices with their start and end apart: 3, of which 3 were waited for; matrix products, arithmetic and copies ran while one was open for 0% of the time, Pallas kernels for 0%

commit v1 on v0

v1 whole, which is shorter than its diff:
```python
import functools

import jax
import jax.numpy as jnp
from jax import lax
from jax.experimental import pallas as pl
from jax.experimental.pallas import tpu as pltpu
from jax.sharding import PartitionSpec as P

ITERS = 3
code_temp = 0.2
loss_temp = 0.3

MESH = pl.DeviceIdType.MESH
F32 = jnp.float32
BF16 = jnp.bfloat16


def snake(p):
    return 2 * (p // 2) + (p + p // 2) % 2


def kernel(
    R, C, feat, protos, out, G, Pb, PT, S, E, SL, GT, fbuf, sendb, st0, st1, a1, a2, b1, b2, q0, q1, res0, res1, wv, av, fv, cs,
    lsem, psend, precv, rs_s, rs_r, ls_s, ls_r, c_s, c_r, x1s, x1r, x2s, x2r, x3s, x3r, gsend, grecv,
):
    NC = R * C // 2
    H = NC // 2
    RC = R // C
    Bl, dl = feat.shape
    hb = Bl // 2
    dr = protos.shape[0]
    kl = protos.shape[1] // R
    ratio = float(Bl * R) / float(protos.shape[1] * C)

    r = lax.axis_index("rows")
    c = lax.axis_index("cls")
    x, core = c // 2, c % 2

    def pos(r_, x_):
        p = snake(r_)
        return x_ * R + jnp.where(x_ % 2 == 0, p, R - 1 - p)

    def place(q_):
        x_ = q_ // R
        p = q_ % R
        return snake(jnp.where(x_ % 2 == 0, p, R - 1 - p)), x_

    q = pos(r, x)
    rr, rx = place((q + 1) % NC)
    lr, lx = place((q + NC - 1) % NC)
    right = (rr, rx * 2 + core)
    left = (lr, lx * 2 + core)
    partner = (r, x * 2 + 1 - core)

    def rpeer(o):
        return (r + o) % R

    def cpeer(o):
        return (c + o) % C

    barrier = pltpu.get_barrier_semaphore()

    def sig_r(o, _):
        pl.semaphore_signal(barrier, inc=1, device_id=(rpeer(o), c), device_id_type=MESH)
        return 0

    def sig_c(o, _):
        pl.semaphore_signal(barrier, inc=1, device_id=(r, cpeer(o)), device_id_type=MESH)
        return 0

    own = pltpu.make_async_copy(feat, G.at[q, core], lsem.at[0])
    own.start()
    lax.fori_loop(1, R, sig_r, 0)
    lax.fori_loop(1, C, sig_c, 0)
    pl.semaphore_wait(barrier, R + C - 2)
    own.wait()

    def half(q_, co, h):
        return G.at[q_, co, pl.ds(h * hb, hb)]

    def ring(s, h, to_right):
        o = (q - s + NC) % NC if to_right else (q + s) % NC
        ss, rs = (rs_s, rs_r) if to_right else (ls_s, ls_r)
        return pltpu.make_async_remote_copy(
            src_ref=half(o, core, h), dst_ref=half(o, core, h), send_sem=ss.at[s, h], recv_sem=rs.at[s, h],
            device_id=right if to_right else left, device_id_type=MESH,
        )

    def pair(d, s, h):
        o = (q - s + NC) % NC if d == 0 else (q + s) % NC
        return pltpu.make_async_remote_copy(
            src_ref=half(o, core, h), dst_ref=half(o, core, h), send_sem=psend.at[d, s, h], recv_sem=precv.at[d, s, h],
            device_id=partner, device_id_type=MESH,
        )

    def pair_in(d, s, h):
        o = (q - s + NC) % NC if d == 0 else (q + s) % NC
        return pltpu.make_async_remote_copy(
            src_ref=half(o, 1 - core, h), dst_ref=half(o, 1 - core, h), send_sem=psend.at[d, s, h], recv_sem=precv.at[d, s, h],
            device_id=partner, device_id_type=MESH,
        )

    for h in (0, 1):
        ring(0, h, True).start()
        ring(0, h, False).start()

    def proto_copy(o, slot_r):
        return pltpu.make_async_remote_copy(
            src_ref=protos.at[:, pl.ds(pl.multiple_of(rpeer(o) * kl, kl), kl)],
            dst_ref=Pb.at[slot_r // RC, pl.ds(pl.multiple_of((slot_r % RC) * dr, dr), dr)],
            send_sem=c_s.at[o], recv_sem=c_r.at[o],
            device_id=(rpeer(o), c), device_id_type=MESH,
        )

    def proto_start(o, _):
        proto_copy(o, r).start()
        return 0

    lax.fori_loop(1, R, proto_start, 0)
    mine = pltpu.make_async_copy(
        protos.at[:, pl.ds(pl.multiple_of(r * kl, kl), kl)],
        Pb.at[r // RC, pl.ds(pl.multiple_of((r % RC) * dr, dr), dr)],
        lsem.at[1],
    )
    mine.start()
    for h in (0, 1):
        pair(0, 0, h).start()

    def zero(i, _):
        S[i] = jnp.zeros(S.shape[1:], F32)
        return 0

    lax.fori_loop(0, R, zero, 0)

    def proto_wait(o, _):
        proto_copy(o, (r - o + R) % R).wait()
        return 0

    lax.fori_loop(1, R, proto_wait, 0)
    mine.wait()

    def turn(i, _):
        PT[i] = Pb[i].astype(F32).T.astype(BF16)
        return 0

    lax.fori_loop(0, C, turn, 0)

    def load(q_, co, slot):
        return pltpu.make_async_copy(G.at[q_, co], fbuf.at[slot], lsem.at[2 + slot])

    def absorb(blocks):
        for i, (q_, co) in enumerate(blocks):
            load(q_, co, i).start()
        for i, (q_, co) in enumerate(blocks):
            load(q_, co, i).wait()
            r_, x_ = place(q_)
            S[r_] += lax.dot_general(
                PT[x_ * 2 + co], fbuf[i], (((1,), (1,)), ((), ())), preferred_element_type=F32
            )

    def behind(s):
        return (q - s + NC) % NC

    def ahead(s):
        return (q + s) % NC

    def ring_step(s, _):
        for h in (0, 1):
            ring(s - 1, h, True).wait_recv()
            ring(s - 1, h, False).wait_recv()

            @pl.when(jnp.logical_or(s < H - 1, h == 0))
            def _():
                ring(s, h, True).start()

            @pl.when(jnp.logical_or(s < H - 1, h == 1))
            def _():
                ring(s, h, False).start()

            pair(0, s, h).start()
            pair(1, s, h).start()
            if h == 0:

                @pl.when(s == 1)
                def _():
                    for hh in (0, 1):
                        pair_in(0, 0, hh).wait_recv()
                    absorb([(q, core), (q, 1 - core)])

                @pl.when(s > 1)
                def _():
                    for hh in (0, 1):
                        pair_in(0, s - 1, hh).wait_recv()
                        pair_in(1, s - 1, hh).wait_recv()
                    absorb([(behind(s - 1), core), (ahead(s - 1), core), (behind(s - 1), 1 - core), (ahead(s - 1), 1 - core)])
        return 0

    lax.fori_loop(1, H, ring_step, 0)
    for hh in (0, 1):
        pair_in(0, H - 1, hh).wait_recv()
        pair_in(1, H - 1, hh).wait_recv()
    absorb(
        [(behind(H - 1), core), (ahead(H - 1), core), (behind(H - 1), 1 - core), (ahead(H - 1), 1 - core)]
    )
    ring(H - 1, 0, True).wait_recv()
    pair(0, H, 0).start()
    ring(H - 1, 1, False).wait_recv()
    pair(1, H, 1).start()
    pair_in(0, H, 0).wait_recv()
    pair_in(1, H, 1).wait_recv()
    absorb([(behind(H), core), (behind(H), 1 - core)])

    def exchange(e, st, s1, s2, qv, res, join):
        def one(o):
            return pltpu.make_async_remote_copy(
                src_ref=st.at[pl.ds(cpeer(o) * RC, RC)], dst_ref=s1.at[c],
                send_sem=x1s.at[e, o], recv_sem=x1r.at[e, o], device_id=(r, cpeer(o)), device_id_type=MESH,
            )

        for o in range(1, C):
            one(o).start()
        s1[c] = st[pl.ds(c * RC, RC)]
        for o in range(1, C):
            one(o).wait()
        qv[...] = join([s1[i] for i in range(C)])

        def two(o):
            return pltpu.make_async_remote_copy(
                src_ref=qv, dst_ref=s2.at[r],
                send_sem=x2s.at[e, o], recv_sem=x2r.at[e, o], device_id=(rpeer(o), c), device_id_type=MESH,
            )

        for o in range(1, R):
            two(o).start()
        s2[r] = qv[...]
        for o in range(1, R):
            two(o).wait()
        res[pl.ds(c * RC, RC)] = join([s2[i] for i in range(R)])

        def three(o):
            return pltpu.make_async_remote_copy(
                src_ref=res.at[pl.ds(c * RC, RC)], dst_ref=res.at[pl.ds(c * RC, RC)],
                send_sem=x3s.at[e, o], recv_sem=x3r.at[e, o], device_id=(r, cpeer(o)), device_id_type=MESH,
            )

        for o in range(1, C):
            three(o).start()
        for o in range(1, C):
            three(o).wait()

    def join_stats(parts):
        top = functools.reduce(jnp.maximum, [p[:, 0] for p in parts])
        s2 = sum(p[:, 1] * jnp.exp((p[:, 0] - top) / code_temp) for p in parts)
        s3 = sum(p[:, 2] * jnp.exp((p[:, 0] - top) / loss_temp) for p in parts)
        return jnp.stack([top, s2, s3], axis=1)

    def join_sum(parts):
        return functools.reduce(jnp.add, parts)

    def first(i, _):
        sc = S[i]
        top = jnp.max(sc, axis=0, keepdims=True)
        sh = sc - top
        e2 = jnp.exp(sh / code_temp)
        e3 = jnp.exp(sh / loss_temp)
        E[i] = e2
        S[i] = e3
        st0[i, 0] = top
        st0[i, 1] = jnp.sum(e2, axis=0, keepdims=True)
        st0[i, 2] = jnp.sum(e3, axis=0, keepdims=True)
        return 0

    lax.fori_loop(0, R, first, 0)
    exchange(0, st0, a1, a2, q0, res0, join_stats)

    def scales(i, _):
        down = st0[i, 0] - res0[i, 0]
        f2 = jnp.exp(down / code_temp)
        fv[i] = f2
        wv[i] = f2 / res0[i, 1]
        av[i] = jnp.exp(down / loss_temp) / res0[i, 2]
        return 0

    lax.fori_loop(0, R, scales, 0)

    for sweep in range(ITERS):

        def col(i, acc):
            m = E[i] * wv[i]
            return acc + functools.reduce(jnp.add, [m[:, j * 128 : (j + 1) * 128] for j in range(Bl // 128)])

        mass = lax.fori_loop(0, R, col, jnp.zeros((kl, 128), F32))
        cs[...] = jnp.broadcast_to(ratio / jnp.sum(mass, axis=1, keepdims=True), (kl, 128))

        def row(i, _):
            st1[sweep, i, 0] = jnp.sum(E[i] * cs[:, 0:1], axis=0, keepdims=True) * fv[i]
            return 0

        lax.fori_loop(0, R, row, 0)
        exchange(sweep + 1, st1.at[sweep], b1.at[sweep], b2.at[sweep], q1.at[sweep], res1.at[sweep], join_sum)

        def rescale(i, _):
            wv[i] = fv[i] / res1[sweep, i, 0]
            return 0

        lax.fori_loop(0, R, rescale, 0)

    def slope(i, _):
        SL[i] = ((S[i] * av[i] - E[i] * wv[i] * cs[:, 0:1]) / loss_temp).astype(BF16)
        return 0

    lax.fori_loop(0, R, slope, 0)

    def block_of(t):
        return (t + 1 + r // RC) % C

    def grad_load(n):
        cb = block_of(n // R)
        return load(pos(n % R, cb // 2), cb % 2, n % 2)

    def grad_copy(t, j, src_r):
        dest = block_of(t) * RC + j
        return pltpu.make_async_remote_copy(
            src_ref=sendb.at[t, pl.ds(pl.multiple_of(j * dr, dr), dr)],
            dst_ref=out.at[:, pl.ds(pl.multiple_of(src_r * kl, kl), kl)],
            send_sem=gsend.at[t, j], recv_sem=grecv.at[src_r],
            device_id=(dest, c), device_id_type=MESH,
        )

    def own_grad():
        return pltpu.make_async_copy(
            sendb.at[C - 1, pl.ds(pl.multiple_of((r % RC) * dr, dr), dr)],
            out.at[:, pl.ds(pl.multiple_of(r * kl, kl), kl)],
            lsem.at[1],
        )

    grad_load(0).start()

    def grad(n, _):
        t = n // R

        @pl.when(n + 1 < R * C)
        def _():
            grad_load(n + 1).start()

        grad_load(n).wait()
        part = jnp.dot(SL[n % R], fbuf[n % 2], preferred_element_type=F32)

        @pl.when(n % R == 0)
        def _():
            GT[...] = part

        @pl.when(n % R > 0)
        def _():
            GT[...] += part

        @pl.when(n % R == R - 1)
        def _():
            sendb[t] = GT[...].T.astype(BF16)
            for j in range(RC):

                @pl.when(block_of(t) * RC + j != r)
                def _():
                    grad_copy(t, j, r).start()

                @pl.when(block_of(t) * RC + j == r)
                def _():
                    own_grad().start()

        return 0

    lax.fori_loop(0, R * C, grad, 0)

    def drain(s, _):
        for h in (0, 1):

            @pl.when(jnp.logical_or(s < H - 1, h == 0))
            def _():
                ring(s, h, True).wait_send()

            @pl.when(jnp.logical_or(s < H - 1, h == 1))
            def _():
                ring(s, h, False).wait_send()

            pair(0, s, h).wait_send()

            @pl.when(s > 0)
            def _():
                pair(1, s, h).wait_send()

        return 0

    lax.fori_loop(0, H, drain, 0)
    pair(0, H, 0).wait_send()
    pair(1, H, 1).wait_send()
    own_grad().wait()

    def sent(n, _):
        @pl.when(block_of(n // RC) * RC + n % RC != r)
        def _():
            grad_copy(n // RC, n % RC, r).wait_send()

        return 0

    lax.fori_loop(0, C * RC, sent, 0)

    def got(o, _):
        grad_copy(0, 0, rpeer(o)).wait_recv()
        return 0

    lax.fori_loop(1, R, got, 0)


def solution(mesh):
    R, C = mesh.shape["rows"], mesh.shape["cls"]

    def local(features, prototypes):
        Bl, dl = features.shape
        dr, kc = prototypes.shape
        kl = kc // R
        NC, RC = R * C // 2, R // C
        H = NC // 2
        X = ITERS + 1
        dma = pltpu.SemaphoreType.DMA
        V = pltpu.VMEM
        out, _ = pl.pallas_call(
            functools.partial(kernel, R, C),
            out_shape=(
                jax.ShapeDtypeStruct((dr, kc), BF16),
                jax.ShapeDtypeStruct((NC, 2, Bl, dl), BF16),
            ),
            in_specs=[pl.BlockSpec(memory_space=pl.ANY)] * 2,
            out_specs=(pl.BlockSpec(memory_space=pl.ANY),) * 2,
            scratch_shapes=[
                V((C, dl, kl), BF16),
                V((C, kl, dl), BF16),
                V((R, kl, Bl), F32),
                V((R, kl, Bl), F32),
                V((R, kl, Bl), BF16),
                V((kl, dl), F32),
                V((4, Bl, dl), BF16),
                V((C, dl, kl), BF16),
                V((R, 3, 1, Bl), F32),
                V((ITERS, R, 1, 1, Bl), F32),
                V((C, RC, 3, 1, Bl), F32),
                V((R, RC, 3, 1, Bl), F32),
                V((ITERS, C, RC, 1, 1, Bl), F32),
                V((ITERS, R, RC, 1, 1, Bl), F32),
                V((RC, 3, 1, Bl), F32),
                V((ITERS, RC, 1, 1, Bl), F32),
                V((R, 3, 1, Bl), F32),
                V((ITERS, R, 1, 1, Bl), F32),
                V((R, 1, Bl), F32),
                V((R, 1, Bl), F32),
                V((R, 1, Bl), F32),
                V((kl, 128), F32),
                dma((6,)),
                dma((2, H + 1, 2)),
                dma((2, H + 1, 2)),
                dma((H, 2)),
                dma((H, 2)),
                dma((H, 2)),
                dma((H, 2)),
                dma((R,)),
                dma((R,)),
                dma((X, C)),
                dma((X, C)),
                dma((X, R)),
                dma((X, R)),
                dma((X, C)),
                dma((X, C)),
                dma((C, RC)),
                dma((R,)),
            ],
            compiler_params=pltpu.CompilerParams(
                collective_id=0, has_side_effects=True, vmem_limit_bytes=60 * 1024 * 1024
            ),
        )(features, prototypes)
        return out.astype(F32)

    return jax.shard_map(
        local,
        mesh=mesh,
        in_specs=(P("rows", "cls"), P("rows", "cls")),
        out_specs=P("rows", "cls"),
        check_vma=False,
    )
```

time: 787 us -> 326 us (0.41)
  waiting for transfers between devices: 540 us -> 0 us
  Pallas kernels: 0 us -> 322 us
  blocking collectives: 130 us -> 0 us
  other arithmetic: 53.1 us -> 4.1 us
  matrix products: 43 us -> 0 us
  between operations: 13.1 us -> 0.01 us
    pallas_call x0 -> x1, Pallas kernels: none -> 322 us  [local(): pl.pallas_call(functools.partial(kernel, R, C), out_shape=(jax.ShapeDtype...]
    reduce_scatter x1 -> x0, waiting for transfers between devices: 281 us -> none  [local(): lax.psum_scatter(lax.dot_general(columns, slope, (((0,), (0,)), ((), ()))...]
    all_gather x2 -> x0, waiting for transfers between devices: 257 us -> none  [the longest x1 226 us: local(): lax.all_gather(prototypes, 'rows', axis=0, tiled=True)]
    psum x7 -> x0, blocking collectives: 124 us -> none  [the longest x3 78 us: local(): col_mass = lax.psum(jnp.sum(codes, axis=0), 'rows')]
    reduce_sum x7 -> x0, other arithmetic: 53.1 us -> none  [the longest x3 29 us: local(): col_mass = lax.psum(jnp.sum(codes, axis=0), 'rows')]
    dot_general x2 -> x0, matrix products: 43 us -> none  [the longest x1 22.6 us: local(): lax.dot_general(columns, slope, (((0,), (0,)), ((), ())), preferred_eleme...]
  transfers between devices with their start and end apart: 3 -> 0, of which waited for: 3 -> 0; matrix products, arithmetic and copies ran while one was open for 0% -> 0% of each run, Pallas kernels for 0% -> 0%
where the time goes in v1:
time: 326 us
  Pallas kernels  322 us (99%)
  other arithmetic  4.1 us (1%)
    pallas_call x1, Pallas kernels, local(): pl.pallas_call(functools.partial(kernel, R, C), out_shape=(jax.ShapeDtype...  322 us

profile of v1, /device:TPU:13, one launch (start us, length us, event | category | flops | bytes accessed | tf_op | source)
XLA Modules:
  0.0 325.7 jit_solution(12226790924737991451)
XLA Ops:
  0.0 321.6 %shard_map.28 = (bf16[256,4096]{1,0:T(8,128)(2,1)}, bf16[16,2,768,512]{3,2,1,0:T(8,128)(2,1)}) custom-call(bf16[768,512]{1,0:T(8,128)(2,1)} %feat.1, bf16[256,4096]{1,0:T(8,128)(2,1)} %protos.1), custom_call_target="tpu_custom_call" | custom-call | tf_op jit(solution)/shard_map/pallas_call | solution.py:427
  321.6 4.1 %convert_element_type.3 = f32[256,4096]{1,0:T(8,128)} convert(bf16[256,4096]{1,0:T(8,128)(2,1)} %get-tuple-element.6) | non-fusion elementwise | flops 1048576 | bytes 6291456 | tf_op jit(solution)/shard_map/convert_element_type | solution.py:480

commit v2 on v1

--- a/solution.py
+++ b/solution.py
@@ -16,16 +16,11 @@
 BF16 = jnp.bfloat16
 
 
-def snake(p):
-    return 2 * (p // 2) + (p + p // 2) % 2
-
-
 def kernel(
     R, C, feat, protos, out, G, Pb, PT, S, E, SL, GT, fbuf, sendb, st0, st1, a1, a2, b1, b2, q0, q1, res0, res1, wv, av, fv, cs,
-    lsem, psend, precv, rs_s, rs_r, ls_s, ls_r, c_s, c_r, x1s, x1r, x2s, x2r, x3s, x3r, gsend, grecv,
+    lsem, ps, pr, up_s, dn_s, ln_r, ns, nr, ds_, dr_, c_s, c_r, x1s, x1r, x2s, x2r, x3s, x3r, gsend, grecv,
 ):
-    NC = R * C // 2
-    H = NC // 2
+    Z = R // 2
     RC = R // C
     Bl, dl = feat.shape
     hb = Bl // 2
@@ -36,21 +31,9 @@
     r = lax.axis_index("rows")
     c = lax.axis_index("cls")
     x, core = c // 2, c % 2
-
-    def pos(r_, x_):
-        p = snake(r_)
-        return x_ * R + jnp.where(x_ % 2 == 0, p, R - 1 - p)
-
-    def place(q_):
-        x_ = q_ // R
-        p = q_ % R
-        return snake(jnp.where(x_ % 2 == 0, p, R - 1 - p)), x_
-
-    q = pos(r, x)
-    rr, rx = place((q + 1) % NC)
-    lr, lx = place((q + NC - 1) % NC)
-    right = (rr, rx * 2 + core)
-    left = (lr, lx * 2 + core)
+    z, y = r // 2, r % 2
+    x_near = (r, (1 - x) * 2 + core)
+    y_near = (2 * z + 1 - y, c)
     partner = (r, x * 2 + 1 - core)
 
     def rpeer(o):
@@ -69,41 +52,106 @@
         pl.semaphore_signal(barrier, inc=1, device_id=(r, cpeer(o)), device_id_type=MESH)
         return 0
 
-    own = pltpu.make_async_copy(feat, G.at[q, core], lsem.at[0])
+    own = pltpu.make_async_copy(feat, G.at[r, c], lsem.at[0])
     own.start()
     lax.fori_loop(1, R, sig_r, 0)
     lax.fori_loop(1, C, sig_c, 0)
     pl.semaphore_wait(barrier, R + C - 2)
     own.wait()
 
-    def half(q_, co, h):
-        return G.at[q_, co, pl.ds(h * hb, hb)]
-
-    def ring(s, h, to_right):
-        o = (q - s + NC) % NC if to_right else (q + s) % NC
-        ss, rs = (rs_s, rs_r) if to_right else (ls_s, ls_r)
+    def half(quad, o, h, co):
+        xq = 1 - x if quad in (1, 3) else x
+        yq = 1 - y if quad in (2, 3) else y
+        return G.at[2 * o + yq, 2 * xq + co, pl.ds(h * hb, hb)]
+
+    def send(src, send_sem, recv_sem, dest):
         return pltpu.make_async_remote_copy(
-            src_ref=half(o, core, h), dst_ref=half(o, core, h), send_sem=ss.at[s, h], recv_sem=rs.at[s, h],
-            device_id=right if to_right else left, device_id_type=MESH,
+            src_ref=src, dst_ref=src, send_sem=send_sem, recv_sem=recv_sem, device_id=dest, device_id_type=MESH
         )
 
-    def pair(d, s, h):
-        o = (q - s + NC) % NC if d == 0 else (q + s) % NC
-        return pltpu.make_async_remote_copy(
-            src_ref=half(o, core, h), dst_ref=half(o, core, h), send_sem=psend.at[d, s, h], recv_sem=precv.at[d, s, h],
-            device_id=partner, device_id_type=MESH,
-        )
-
-    def pair_in(d, s, h):
-        o = (q - s + NC) % NC if d == 0 else (q + s) % NC
-        return pltpu.make_async_remote_copy(
-            src_ref=half(o, 1 - core, h), dst_ref=half(o, 1 - core, h), send_sem=psend.at[d, s, h], recv_sem=precv.at[d, s, h],
-            device_id=partner, device_id_type=MESH,
-        )
-
-    for h in (0, 1):
-        ring(0, h, True).start()
-        ring(0, h, False).start()
+    def line_up(o, h):
+        return send(half(0, o, h, core), up_s.at[o, h], ln_r.at[o, h], (r + 2, c))
+
+    def line_down(o, h):
+        return send(half(0, o, h, core), dn_s.at[o, h], ln_r.at[o, h], (r - 2, c))
+
+    def line_in(o, h):
+        return send(half(0, o, h, core), up_s.at[o, h], ln_r.at[o, h], partner)
+
+    def near(axis, o, h):
+        return send(half(0, o, h, core), ns.at[axis, o, h], nr.at[axis, o, h], (x_near, y_near)[axis])
+
+    def near_in(axis, o, h):
+        return send(half(1 + axis, o, h, core), ns.at[axis, o, h], nr.at[axis, o, h], (x_near, y_near)[axis])
+
+    def diag(h, o):
+        return send(half(2 - h, o, h, core), ds_.at[o, h], dr_.at[o, h], (x_near, y_near)[h])
+
+    def diag_in(h, o):
+        return send(half(3, o, h, core), ds_.at[o, h], dr_.at[o, h], (x_near, y_near)[h])
+
+    def pair(quad, o, h):
+        return send(half(quad, o, h, core), ps.at[quad, o, h], pr.at[quad, o, h], partner)
+
+    def pair_in(quad, o, h):
+        return send(half(quad, o, h, 1 - core), ps.at[quad, o, h], pr.at[quad, o, h], partner)
+
+    def sides(k, fn):
+        if isinstance(k, int) and k == 0:
+            fn(z, None)
+            return
+
+        @pl.when(z - k >= 0)
+        def _():
+            fn(z - k, 0)
+
+        @pl.when(z + k < Z)
+        def _():
+            fn(z + k, 1)
+
+    def do_line(k):
+        def step(o, side):
+            for h in (0, 1):
+                if side is not None:
+                    line_in(o, h).wait_recv()
+                if side != 1:
+
+                    @pl.when(z + 1 < Z)
+                    def _():
+                        line_up(o, h).start()
+
+                if side != 0:
+
+                    @pl.when(z >= 1)
+                    def _():
+                        line_down(o, h).start()
+
+                near(0, o, h).start()
+                near(1, o, h).start()
+                pair(0, o, h).start()
+
+        sides(k, step)
+
+    def do_near(k):
+        def step(o, side):
+            for h in (0, 1):
+                for axis in (1, 0):
+                    near_in(axis, o, h).wait_recv()
+                    if axis == 1 - h:
+                        diag(h, o).start()
+                    pair(1 + axis, o, h).start()
+
+        sides(k, step)
+
+    def do_diag(k):
+        def step(o, side):
+            for h in (0, 1):
+                diag_in(h, o).wait_recv()
+                pair(3, o, h).start()
+
+        sides(k, step)
+
+    do_line(0)
 
     def proto_copy(o, slot_r):
         return pltpu.make_async_remote_copy(
@@ -124,9 +172,6 @@
         lsem.at[1],
     )
     mine.start()
-    for h in (0, 1):
-        pair(0, 0, h).start()
-
     def zero(i, _):
         S[i] = jnp.zeros(S.shape[1:], F32)
         return 0
@@ -146,70 +191,56 @@
 
     lax.fori_loop(0, C, turn, 0)
 
-    def load(q_, co, slot):
-        return pltpu.make_async_copy(G.at[q_, co], fbuf.at[slot], lsem.at[2 + slot])
-
-    def absorb(blocks):
-        for i, (q_, co) in enumerate(blocks):
-            load(q_, co, i).start()
-        for i, (q_, co) in enumerate(blocks):
-            load(q_, co, i).wait()
-            r_, x_ = place(q_)
-            S[r_] += lax.dot_general(
-                PT[x_ * 2 + co], fbuf[i], (((1,), (1,)), ((), ())), preferred_element_type=F32
-            )
-
-    def behind(s):
-        return (q - s + NC) % NC
-
-    def ahead(s):
-        return (q + s) % NC
-
-    def ring_step(s, _):
-        for h in (0, 1):
-            ring(s - 1, h, True).wait_recv()
-            ring(s - 1, h, False).wait_recv()
-
-            @pl.when(jnp.logical_or(s < H - 1, h == 0))
-            def _():
-                ring(s, h, True).start()
-
-            @pl.when(jnp.logical_or(s < H - 1, h == 1))
-            def _():
-                ring(s, h, False).start()
-
-            pair(0, s, h).start()
-            pair(1, s, h).start()
-            if h == 0:
-
-                @pl.when(s == 1)
-                def _():
-                    for hh in (0, 1):
-                        pair_in(0, 0, hh).wait_recv()
-                    absorb([(q, core), (q, 1 - core)])
-
-                @pl.when(s > 1)
-                def _():
-                    for hh in (0, 1):
-                        pair_in(0, s - 1, hh).wait_recv()
-                        pair_in(1, s - 1, hh).wait_recv()
-                    absorb([(behind(s - 1), core), (ahead(s - 1), core), (behind(s - 1), 1 - core), (ahead(s - 1), 1 - core)])
-        return 0
-
-    lax.fori_loop(1, H, ring_step, 0)
-    for hh in (0, 1):
-        pair_in(0, H - 1, hh).wait_recv()
-        pair_in(1, H - 1, hh).wait_recv()
-    absorb(
-        [(behind(H - 1), core), (ahead(H - 1), core), (behind(H - 1), 1 - core), (ahead(H - 1), 1 - core)]
-    )
-    ring(H - 1, 0, True).wait_recv()
-    pair(0, H, 0).start()
-    ring(H - 1, 1, False).wait_recv()
-    pair(1, H, 1).start()
-    pair_in(0, H, 0).wait_recv()
-    pair_in(1, H, 1).wait_recv()
-    absorb([(behind(H), core), (behind(H), 1 - core)])
+    def load(r_, c_, slot):
+        return pltpu.make_async_copy(G.at[r_, c_], fbuf.at[slot], lsem.at[2 + slot])
+
+    def absorb(quads, k):
+        def step(o, side):
+            blocks = []
+            for quad in quads:
+                for h in (0, 1):
+                    pair_in(quad, o, h).wait_recv()
+                xq = 1 - x if quad in (1, 3) else x
+                yq = 1 - y if quad in (2, 3) else y
+                blocks += [(2 * o + yq, 2 * xq + core), (2 * o + yq, 2 * xq + 1 - core)]
+            for i, (r_, c_) in enumerate(blocks):
+                load(r_, c_, i).start()
+            for i, (r_, c_) in enumerate(blocks):
+                load(r_, c_, i).wait()
+                S[r_] += lax.dot_general(PT[c_], fbuf[i], (((1,), (1,)), ((), ())), preferred_element_type=F32)
+
+        sides(k, step)
+
+    do_line(1)
+    do_near(0)
+    absorb((0,), 0)
+
+    def later(k, _):
+        @pl.when(k < Z)
+        def _():
+            do_line(k)
+
+        do_near(k - 1)
+        absorb((0,), k - 1)
+
+        @pl.when(k == 2)
+        def _():
+            do_diag(0)
+            absorb((1, 2), 0)
+            absorb((3,), 0)
+
+        @pl.when(k > 2)
+        def _():
+            do_diag(k - 2)
+            absorb((1, 2), k - 2)
+            absorb((3,), k - 2)
+
+        return 0
+
+    lax.fori_loop(2, Z + 1, later, 0)
+    absorb((1, 2), Z - 1)
+    do_diag(Z - 1)
+    absorb((3,), Z - 1)
 
     def exchange(e, st, s1, s2, qv, res, join):
         def one(o):
@@ -313,11 +344,12 @@
     lax.fori_loop(0, R, slope, 0)
 
     def block_of(t):
-        return (t + 1 + r // RC) % C
+        g = r // RC
+        return (2 * (g // 2) + 2 * (1 - t // 2)) % 4 + (g + 1 - t % 2) % 2
 
     def grad_load(n):
         cb = block_of(n // R)
-        return load(pos(n % R, cb // 2), cb % 2, n % 2)
+        return load(n % R, cb, n % 2)
 
     def grad_copy(t, j, src_r):
         dest = block_of(t) * RC + j
@@ -372,28 +404,26 @@
 
     lax.fori_loop(0, R * C, grad, 0)
 
-    def drain(s, _):
+    def drain(o, _):
         for h in (0, 1):
 
-            @pl.when(jnp.logical_or(s < H - 1, h == 0))
+            @pl.when(jnp.logical_and(o <= z, z + 1 < Z))
             def _():
-                ring(s, h, True).wait_send()
-
-            @pl.when(jnp.logical_or(s < H - 1, h == 1))
+                line_up(o, h).wait_send()
+
+            @pl.when(jnp.logical_and(o >= z, z >= 1))
             def _():
-                ring(s, h, False).wait_send()
-
-            pair(0, s, h).wait_send()
-
-            @pl.when(s > 0)
-            def _():
-                pair(1, s, h).wait_send()
-
-        return 0
-
-    lax.fori_loop(0, H, drain, 0)
-    pair(0, H, 0).wait_send()
-    pair(1, H, 1).wait_send()
+                line_down(o, h).wait_send()
+
+            near(0, o, h).wait_send()
+            near(1, o, h).wait_send()
+            diag(h, o).wait_send()
+            for quad in range(4):
+                pair(quad, o, h).wait_send()
+
+        return 0
+
+    lax.fori_loop(0, Z, drain, 0)
     own_grad().wait()
 
     def sent(n, _):
@@ -414,13 +444,13 @@
 
 def solution(mesh):
     R, C = mesh.shape["rows"], mesh.shape["cls"]
+    assert C == 4 and R % 4 == 0
 
     def local(features, prototypes):
         Bl, dl = features.shape
         dr, kc = prototypes.shape
         kl = kc // R
-        NC, RC = R * C // 2, R // C
-        H = NC // 2
+        Z, RC = R // 2, R // C
         X = ITERS + 1
         dma = pltpu.SemaphoreType.DMA
         V = pltpu.VMEM
@@ -428,7 +458,7 @@
             functools.partial(kernel, R, C),
             out_shape=(
                 jax.ShapeDtypeStruct((dr, kc), BF16),
-                jax.ShapeDtypeStruct((NC, 2, Bl, dl), BF16),
+                jax.ShapeDtypeStruct((R, C, Bl, dl), BF16),
             ),
             in_specs=[pl.BlockSpec(memory_space=pl.ANY)] * 2,
             out_specs=(pl.BlockSpec(memory_space=pl.ANY),) * 2,
@@ -456,12 +486,15 @@
                 V((R, 1, Bl), F32),
                 V((kl, 128), F32),
                 dma((6,)),
-                dma((2, H + 1, 2)),
-                dma((2, H + 1, 2)),
-                dma((H, 2)),
-                dma((H, 2)),
-                dma((H, 2)),
-                dma((H, 2)),
+                dma((4, Z, 2)),
+                dma((4, Z, 2)),
+                dma((Z, 2)),
+                dma((Z, 2)),
+                dma((Z, 2)),
+                dma((2, Z, 2)),
+                dma((2, Z, 2)),
+                dma((Z, 2)),
+                dma((Z, 2)),
                 dma((R,)),
                 dma((R,)),
                 dma((X, C)),

time: 326 us -> 312 us (0.957); the launches traced: 326 us -> 307 us
  Pallas kernels: 322 us -> 303 us
    pallas_call x1, Pallas kernels: 322 us -> 303 us  [local(): pl.pallas_call(functools.partial(kernel, R, C), out_shape=(jax.ShapeDtype...]
where the time goes in v2:
time: 312 us; the launch traced here: 307 us
  Pallas kernels  303 us (97%)
  other arithmetic  4.1 us (1%)
    pallas_call x1, Pallas kernels, local(): pl.pallas_call(functools.partial(kernel, R, C), out_shape=(jax.ShapeDtype...  303 us

profile of v2, /device:TPU:13, one launch (start us, length us, event | category | flops | bytes accessed | tf_op | source)
XLA Modules:
  0.0 307.5 jit_solution(7071215270828074678)
XLA Ops:
  0.0 303.4 %shard_map.28 = (bf16[256,4096]{1,0:T(8,128)(2,1)}, bf16[8,4,768,512]{3,2,1,0:T(8,128)(2,1)}) custom-call(bf16[768,512]{1,0:T(8,128)(2,1)} %feat.1, bf16[256,4096]{1,0:T(8,128)(2,1)} %protos.1), custom_call_target="tpu_custom_call" | custom-call | tf_op jit(solution)/shard_map/pallas_call | solution.py:457
  303.4 4.1 %convert_element_type.3 = f32[256,4096]{1,0:T(8,128)} convert(bf16[256,4096]{1,0:T(8,128)(2,1)} %get-tuple-element.6) | non-fusion elementwise | flops 1048576 | bytes 6291456 | tf_op jit(solution)/shard_map/convert_element_type | solution.py:513

commit v3 on v2

--- a/solution.py
+++ b/solution.py
@@ -57,29 +57,28 @@
     lax.fori_loop(1, R, sig_r, 0)
     lax.fori_loop(1, C, sig_c, 0)
     pl.semaphore_wait(barrier, R + C - 2)
-    own.wait()
 
     def half(quad, o, h, co):
         xq = 1 - x if quad in (1, 3) else x
         yq = 1 - y if quad in (2, 3) else y
         return G.at[2 * o + yq, 2 * xq + co, pl.ds(h * hb, hb)]
 
-    def send(src, send_sem, recv_sem, dest):
+    def send(dst, send_sem, recv_sem, dest, src=None):
         return pltpu.make_async_remote_copy(
-            src_ref=src, dst_ref=src, send_sem=send_sem, recv_sem=recv_sem, device_id=dest, device_id_type=MESH
+            src_ref=dst if src is None else src, dst_ref=dst, send_sem=send_sem, recv_sem=recv_sem, device_id=dest, device_id_type=MESH
         )
 
-    def line_up(o, h):
-        return send(half(0, o, h, core), up_s.at[o, h], ln_r.at[o, h], (r + 2, c))
-
-    def line_down(o, h):
-        return send(half(0, o, h, core), dn_s.at[o, h], ln_r.at[o, h], (r - 2, c))
+    def line_up(o, h, src=None):
+        return send(half(0, o, h, core), up_s.at[o, h], ln_r.at[o, h], (r + 2, c), src)
+
+    def line_down(o, h, src=None):
+        return send(half(0, o, h, core), dn_s.at[o, h], ln_r.at[o, h], (r - 2, c), src)
 
     def line_in(o, h):
         return send(half(0, o, h, core), up_s.at[o, h], ln_r.at[o, h], partner)
 
-    def near(axis, o, h):
-        return send(half(0, o, h, core), ns.at[axis, o, h], nr.at[axis, o, h], (x_near, y_near)[axis])
+    def near(axis, o, h, src=None):
+        return send(half(0, o, h, core), ns.at[axis, o, h], nr.at[axis, o, h], (x_near, y_near)[axis], src)
 
     def near_in(axis, o, h):
         return send(half(1 + axis, o, h, core), ns.at[axis, o, h], nr.at[axis, o, h], (x_near, y_near)[axis])
@@ -90,8 +89,8 @@
     def diag_in(h, o):
         return send(half(3, o, h, core), ds_.at[o, h], dr_.at[o, h], (x_near, y_near)[h])
 
-    def pair(quad, o, h):
-        return send(half(quad, o, h, core), ps.at[quad, o, h], pr.at[quad, o, h], partner)
+    def pair(quad, o, h, src=None):
+        return send(half(quad, o, h, core), ps.at[quad, o, h], pr.at[quad, o, h], partner, src)
 
     def pair_in(quad, o, h):
         return send(half(quad, o, h, 1 - core), ps.at[quad, o, h], pr.at[quad, o, h], partner)
@@ -112,23 +111,24 @@
     def do_line(k):
         def step(o, side):
             for h in (0, 1):
+                src = feat.at[pl.ds(h * hb, hb)] if side is None else None
                 if side is not None:
                     line_in(o, h).wait_recv()
                 if side != 1:
 
                     @pl.when(z + 1 < Z)
                     def _():
-                        line_up(o, h).start()
+                        line_up(o, h, src).start()
 
                 if side != 0:
 
                     @pl.when(z >= 1)
                     def _():
-                        line_down(o, h).start()
-
-                near(0, o, h).start()
-                near(1, o, h).start()
-                pair(0, o, h).start()
+                        line_down(o, h, src).start()
+
+                near(0, o, h, src).start()
+                near(1, o, h, src).start()
+                pair(0, o, h, src).start()
 
         sides(k, step)
 
@@ -182,14 +182,15 @@
         proto_copy(o, (r - o + R) % R).wait()
         return 0
 
-    lax.fori_loop(1, R, proto_wait, 0)
-    mine.wait()
-
     def turn(i, _):
         PT[i] = Pb[i].astype(F32).T.astype(BF16)
         return 0
 
-    lax.fori_loop(0, C, turn, 0)
+    def prepare():
+        lax.fori_loop(1, R, proto_wait, 0)
+        mine.wait()
+        lax.fori_loop(0, C, turn, 0)
+        own.wait()
 
     def load(r_, c_, slot):
         return pltpu.make_async_copy(G.at[r_, c_], fbuf.at[slot], lsem.at[2 + slot])
@@ -213,7 +214,6 @@
 
     do_line(1)
     do_near(0)
-    absorb((0,), 0)
 
     def later(k, _):
         @pl.when(k < Z)
@@ -221,13 +221,16 @@
             do_line(k)
 
         do_near(k - 1)
-        absorb((0,), k - 1)
 
         @pl.when(k == 2)
         def _():
             do_diag(0)
+            prepare()
+            absorb((0,), 0)
             absorb((1, 2), 0)
             absorb((3,), 0)
+
+        absorb((0,), k - 1)
 
         @pl.when(k > 2)
         def _():

time: 312 us -> 263 us (0.84)
  Pallas kernels: 303 us -> 255 us
    pallas_call x1, Pallas kernels: 303 us -> 255 us  [local(): pl.pallas_call(functools.partial(kernel, R, C), out_shape=(jax.ShapeDtype...]
where the time goes in v3:
time: 263 us; the launch traced here: 259 us
  Pallas kernels  255 us (97%)
  other arithmetic  4.1 us (2%)
    pallas_call x1, Pallas kernels, local(): pl.pallas_call(functools.partial(kernel, R, C), out_shape=(jax.ShapeDtype...  255 us

profile of v3, /device:TPU:13, one launch (start us, length us, event | category | flops | bytes accessed | tf_op | source)
XLA Modules:
  0.0 259.2 jit_solution(16706505374914789738)
XLA Ops:
  0.0 255.1 %shard_map.28 = (bf16[256,4096]{1,0:T(8,128)(2,1)}, bf16[8,4,768,512]{3,2,1,0:T(8,128)(2,1)}) custom-call(bf16[768,512]{1,0:T(8,128)(2,1)} %feat.1, bf16[256,4096]{1,0:T(8,128)(2,1)} %protos.1), custom_call_target="tpu_custom_call" | custom-call | tf_op jit(solution)/shard_map/pallas_call | solution.py:460
  255.1 4.1 %convert_element_type.3 = f32[256,4096]{1,0:T(8,128)} convert(bf16[256,4096]{1,0:T(8,128)(2,1)} %get-tuple-element.6) | non-fusion elementwise | flops 1048576 | bytes 6291456 | tf_op jit(solution)/shard_map/convert_element_type | solution.py:516

commit v4 on v3

--- a/solution.py
+++ b/solution.py
@@ -165,7 +165,6 @@
         proto_copy(o, r).start()
         return 0
 
-    lax.fori_loop(1, R, proto_start, 0)
     mine = pltpu.make_async_copy(
         protos.at[:, pl.ds(pl.multiple_of(r * kl, kl), kl)],
         Pb.at[r // RC, pl.ds(pl.multiple_of((r % RC) * dr, dr), dr)],
@@ -213,6 +212,7 @@
         sides(k, step)
 
     do_line(1)
+    lax.fori_loop(1, R, proto_start, 0)
     do_near(0)
 
     def later(k, _):

time: 263 us -> 265 us (level)
  no operation moved by 1% of the time
where the time goes in v4:
time: 265 us; the launch traced here: 261 us
  Pallas kernels  256 us (97%)
  other arithmetic  4.1 us (2%)
    pallas_call x1, Pallas kernels, local(): pl.pallas_call(functools.partial(kernel, R, C), out_shape=(jax.ShapeDtype...  256 us

profile of v4, /device:TPU:13, one launch (start us, length us, event | category | flops | bytes accessed | tf_op | source)
XLA Modules:
  0.0 260.5 jit_solution(14657905620657862499)
XLA Ops:
  0.0 256.4 %shard_map.28 = (bf16[256,4096]{1,0:T(8,128)(2,1)}, bf16[8,4,768,512]{3,2,1,0:T(8,128)(2,1)}) custom-call(bf16[768,512]{1,0:T(8,128)(2,1)} %feat.1, bf16[256,4096]{1,0:T(8,128)(2,1)} %protos.1), custom_call_target="tpu_custom_call" | custom-call | tf_op jit(solution)/shard_map/pallas_call | solution.py:460
  256.4 4.1 %convert_element_type.3 = f32[256,4096]{1,0:T(8,128)} convert(bf16[256,4096]{1,0:T(8,128)(2,1)} %get-tuple-element.6) | non-fusion elementwise | flops 1048576 | bytes 6291456 | tf_op jit(solution)/shard_map/convert_element_type | solution.py:516
